TPU v7x, 512 devices: a whole 4x4x16 slice. The times are simulated.
512 devices in a mesh: group: 64 (over x_lo, z, core), shard: 8 (over y, x_hi).
Axes of the slice: x: 4 (x_hi: 2, x_lo: 2; x = x_hi * 2 + x_lo), y: 4, z: 16, core: 2. Of those that a mesh axis runs over, the one named last changes fastest.
Arguments:
- prompts: bfloat16 [512, 128, 1280], P(('group', 'shard')), may hold values from -6 to 6
- lengths: int32 [512], P(('group', 'shard')), may hold values from 32 to 128
- qkv_master: float32 [1280, 1920], P('group', 'shard')
- out_master: float32 [1280, 1280], P('group', 'shard'), may hold values from -0.15625 to 0.15625
- gate_up_master: float32 [1280, 2, 3584], P('group', None, 'shard'), may hold values from -0.15625 to 0.15625
- down_weight: bfloat16 [3584, 1280], P('shard'), may hold values from -0.09375 to 0.09375
- attn_gain: float32 [1280], replicated, may hold values from 0.25 to 1.75
- mlp_gain: float32 [1280], replicated, may hold values from 0.25 to 1.75
Outputs:
- hidden: bfloat16 [512, 128, 1280], P(('group', 'shard'))
- cache: bfloat16 [512, 128, 640], P(('group', 'shard'))
Inputs may be any that keep to these rules, and one draw needn't show every extreme that they name: `lengths`: live tokens of each prompt; positions from the length on are padding.
All inputs are finite; a program needn't handle non-finite values.
Results may differ from a plain program's by a relative error of at most 0.013.
The roundings to bfloat16 on the way count: a program that leaves them out, or rounds other values in their place, can miss the bound.
Values may be sent and summed in bfloat16 or wider, within the bound.
No kernel may reach another device: no remote copies, remote signals or barrier semaphores. Data moves between devices by JAX's collectives and lax.ppermute only.
A program may use at most 64 MiB of HBM per device.

v0:
```python
import jax
import jax.numpy as jnp
from jax import lax
from jax.sharding import PartitionSpec as P

QUERY_HEADS = 20
KEY_VALUE_HEADS = 5
HEAD_SIZE = 64


def norm_rows(stream, scale_gain):
    return (
        stream * lax.rsqrt(jnp.mean(stream * stream, axis=-1, keepdims=True) + 1e-05) * scale_gain
    )


def rotary(heads, positions):
    half_dim = heads.shape[-1] // 2
    frequency = 10000.0 ** (-(jnp.arange(half_dim).astype(heads.dtype) * 2.0 / heads.shape[-1]))
    angles = positions[:, None] * frequency[None, :]
    cosine = jnp.cos(angles)[:, None, :]
    sine_part = jnp.sin(angles)[:, None, :]
    first_half = heads[..., :half_dim]
    second_half = heads[..., half_dim:]
    return jnp.concatenate(
        [
            first_half * cosine - second_half * sine_part,
            second_half * cosine + first_half * sine_part,
        ],
        axis=-1,
    )


def attention(query_key_value, length):
    token_rows = query_key_value.shape[0]
    query = (
        query_key_value[:, : QUERY_HEADS * HEAD_SIZE]
        .astype(jnp.float32)
        .reshape(token_rows, QUERY_HEADS, HEAD_SIZE)
    )
    key_rows = (
        query_key_value[:, QUERY_HEADS * HEAD_SIZE : (QUERY_HEADS + KEY_VALUE_HEADS) * HEAD_SIZE]
        .astype(jnp.float32)
        .reshape(token_rows, KEY_VALUE_HEADS, HEAD_SIZE)
    )
    value_rows = query_key_value[:, (QUERY_HEADS + KEY_VALUE_HEADS) * HEAD_SIZE :].reshape(
        token_rows, KEY_VALUE_HEADS, HEAD_SIZE
    )
    positions = jnp.arange(token_rows).astype(jnp.float32)
    rotated_query = rotary(query, positions).astype(jnp.bfloat16)
    rotated_keys = rotary(key_rows, positions).astype(jnp.bfloat16)
    grouped_queries = rotated_query.reshape(
        token_rows, KEY_VALUE_HEADS, QUERY_HEADS // KEY_VALUE_HEADS, HEAD_SIZE
    )
    scores = jnp.einsum(
        "qkgd,skd->kgqs", grouped_queries, rotated_keys, preferred_element_type=jnp.float32
    ) * HEAD_SIZE ** (-0.5)
    indices = jnp.arange(token_rows)
    allowed = (indices[None, :] <= indices[:, None]) & (indices[None, :] < length)
    scores = jnp.where(allowed, scores, -1e30)
    largest = jnp.max(scores, axis=-1, keepdims=True)
    weights = jnp.exp(scores - largest)
    probability = (weights / jnp.sum(weights, axis=-1, keepdims=True)).astype(jnp.bfloat16)
    attended = jnp.einsum(
        "kgqs,skd->qkgd", probability, value_rows, preferred_element_type=jnp.float32
    )
    return (
        attended.reshape(token_rows, QUERY_HEADS * HEAD_SIZE).astype(jnp.bfloat16),
        rotated_keys,
        value_rows,
    )


def fold_rows(left, blocks):
    summed = jnp.dot(left, blocks[0], preferred_element_type=jnp.float32)
    placed = blocks[1]
    return (summed, placed)


def fold_units(left, block_rows):
    span_rows = block_rows.shape[0]
    return jnp.dot(left, block_rows.reshape(span_rows, -1), preferred_element_type=jnp.float32)


def shards(
    prompts, lengths, qkv_master, out_master, gate_up_master, down_weight, attn_gain, mlp_gain
):
    stream = prompts[0].astype(jnp.float32)
    token_rows = stream.shape[0]
    length = lengths[0]
    normed_in = norm_rows(stream, attn_gain).astype(jnp.bfloat16)
    qkv_columns, out_columns = (
        lax.all_gather(qkv_master.astype(jnp.bfloat16), "shard", axis=1, tiled=True),
        lax.all_gather(out_master.astype(jnp.bfloat16), "shard", axis=1, tiled=True),
    )
    summed, w_out = fold_rows(
        normed_in,
        (
            lax.all_gather(qkv_columns, "group", axis=0, tiled=True),
            lax.all_gather(out_columns, "group", axis=0, tiled=True),
        ),
    )
    query_key_value = summed.astype(jnp.bfloat16)
    attended, rotated_keys, value_rows = attention(query_key_value, length)
    middle = stream + jnp.dot(attended, w_out, preferred_element_type=jnp.float32)
    normed_mid = norm_rows(middle, mlp_gain).astype(jnp.bfloat16)
    gathered_mid = lax.all_gather(normed_mid, "shard", axis=0, tiled=True)
    units = gate_up_master.shape[2]
    summed_units = fold_units(
        gathered_mid,
        lax.all_gather(gate_up_master.astype(jnp.bfloat16), "group", axis=0, tiled=True),
    )
    gate_up = summed_units.reshape(-1, 2, units)
    hidden_units = (jax.nn.silu(gate_up[:, 0]) * gate_up[:, 1]).astype(jnp.bfloat16)
    feed_out = lax.psum_scatter(
        jnp.dot(hidden_units, down_weight, preferred_element_type=jnp.float32).astype(jnp.bfloat16),
        "shard",
        scatter_dimension=0,
        tiled=True,
    ).astype(jnp.float32)
    live_rows = (jnp.arange(token_rows) < length).astype(jnp.float32)[:, None]
    hidden = (live_rows * (middle + feed_out)).astype(jnp.bfloat16)
    joined_heads = jnp.concatenate(
        [
            rotated_keys.reshape(token_rows, KEY_VALUE_HEADS * HEAD_SIZE).astype(jnp.float32),
            value_rows.reshape(token_rows, KEY_VALUE_HEADS * HEAD_SIZE).astype(jnp.float32),
        ],
        axis=-1,
    )
    cache = (live_rows * joined_heads).astype(jnp.bfloat16)
    return (hidden[None], cache[None])


def solution(mesh):
    in_specs = (
        P(("group", "shard"), None, None),
        P(("group", "shard")),
        P("group", "shard"),
        P("group", "shard"),
        P("group", None, "shard"),
        P("shard", None),
        P(),
        P(),
    )
    out_specs = (P(("group", "shard"), None, None), P(("group", "shard"), None, None))
    return jax.shard_map(shards, mesh=mesh, in_specs=in_specs, out_specs=out_specs, check_vma=False)
```

profile of v0, /device:TPU:32, one launch (start us, length us, event | category | flops | bytes accessed | tf_op | source)
XLA Modules:
  0.0 599.7 jit_solution(9727599761350218476)
XLA Ops:
  7.2 0.8 convert_bitcast_fusion
  8.1 34.6 %all-gather.2 = bf16[8,160,20]{1,2,0:T(8,128)(2,1)S(1)} all-gather(bf16[1,160,20]{1,2,0:T(8,128)(2,1)S(1)} %convert_bitcast_fusion), channel_id=1, replica_groups=mesh['group'=64,'shard'=8] {'shard'}, dimensions={0}, use_global_device_ids=true | all-gather | bytes 57600 | tf_op jit(solution)/shard_map/all_gather | solution.py:94
  42.6 0.8 reshape.195
  43.4 0.0 all-gather.13.cloned.1.call-start
  43.5 0.7 convert_bitcast_fusion.1
  44.2 34.2 %all-gather = bf16[8,240,20]{1,2,0:T(8,128)(2,1)S(1)} all-gather(bf16[1,240,20]{1,2,0:T(8,128)(2,1)S(1)} %convert_bitcast_fusion.1), channel_id=1, replica_groups=mesh['group'=64,'shard'=8] {'shard'}, dimensions={0}, use_global_device_ids=true | all-gather | bytes 86400 | tf_op jit(solution)/shard_map/all_gather | solution.py:93
  78.5 0.8 reshape.191
  79.3 0.0 all-gather.11.cloned.1.call-start
  79.3 1.5 convert_element_type.147
  81.6 1.1 fusion.12
  82.8 0.1 fusion.33
  82.9 0.1 multiply_cosine_fusion
  83.0 88.6 %all-gather.15.cloned.1.call-done = bf16[64,20,1280]{2,1,0:T(8,128)(2,1)} async-done(((bf16[1,20,1280]{2,1,0:T(8,128)(2,1)}), bf16[64,20,1280]{2,1,0:T(8,128)(2,1)}) %all-gather.15.cloned.1.call-update) | async-done | bytes 3276816 | tf_op jit(solution)/shard_map/all_gather | solution.py:100
  171.6 6.1 %reshape.197 = bf16[1280,1280]{1,0:T(8,128)(2,1)} reshape(bf16[64,20,1280]{2,1,0:T(8,128)(2,1)} %all-gather.15.cloned.1.call-done) | data formatting | bytes 6553600
  177.7 119.4 %all-gather.13.cloned.1.call-done = bf16[64,20,1920]{2,1,0:T(8,128)(2,1)} async-done(((bf16[1,20,1920]{2,1,0:T(8,128)(2,1)}), bf16[64,20,1920]{2,1,0:T(8,128)(2,1)}) %all-gather.13.cloned.1.call-update) | async-done | bytes 4915216 | tf_op jit(solution)/shard_map/all_gather | solution.py:99
  297.1 7.5 %reshape.193 = bf16[1280,1920]{1,0:T(8,128)(2,1)} reshape(bf16[64,20,1920]{2,1,0:T(8,128)(2,1)} %all-gather.13.cloned.1.call-done) | data formatting | bytes 9830400
  304.7 4.4 convolution_convert_fusion.1
  309.2 0.1 convert.18
  309.3 0.1 subtract_convert_fusion
  309.4 1.7 fusion.41
  311.1 1.7 convolution_convert_fusion.2
  312.8 0.6 copy-done.1
  313.4 0.7 multiply_reduce_fusion
  314.2 0.9 multiply_convert_fusion.1
  315.1 103.7 %all-gather.11.cloned.1.call-done = bf16[1280,2,448]{2,1,0:T(2,128)(2,1)} async-done(((bf16[20,2,448]{2,1,0:T(2,128)(2,1)}), bf16[1280,2,448]{2,1,0:T(2,128)(2,1)}) %all-gather.11.cloned.1.call-update) | async-done | bytes 2293776 | tf_op jit(solution)/shard_map/all_gather | solution.py:111
  418.8 7.4 %copy.40 = bf16[1280,2,448]{0,2,1:T(8,128)(2,1)} copy(bf16[1280,2,448]{2,1,0:T(2,128)(2,1)} %all-gather.11.cloned.1.call-done) | data formatting | bytes 4587520 | tf_op jit(solution)/shard_map/all_gather | solution.py:111
  426.2 66.2 %all-gather.9.cloned.1.call-done = bf16[1024,1280]{1,0:T(8,128)(2,1)} async-done(((bf16[128,1280]{1,0:T(8,128)(2,1)}), bf16[1024,1280]{1,0:T(8,128)(2,1)}) %all-gather.9.cloned.1.call-update) | async-done | bytes 2621456 | tf_op jit(solution)/shard_map/all_gather | solution.py:107
  492.4 5.0 fusion.1
  497.4 3.2 convolution_convert_fusion
  500.7 0.8 copy.41
  501.5 89.9 %reduce-scatter.2.cloned.1.call-done = bf16[128,1280]{1,0:T(8,128)(2,1)} async-done(((bf16[1024,1280]{1,0:T(8,128)(2,1)}), bf16[128,1280]{1,0:T(8,128)(2,1)}) %reduce-scatter.2.cloned.1.call-update) | async-done | bytes 327696 | tf_op jit(solution)/shard_map/reduce_scatter | solution.py:115
  591.4 1.8 fusion.15
  (31 shorter events, 0.4 us)
Async XLA Ops:
  7.2 490.2 %copy-start = (bf16[448,1280]{1,0:T(8,128)(2,1)S(1)}, bf16[448,1280]{1,0:T(8,128)(2,1)}, u32[]{:S(2)}) copy-start(bf16[448,1280]{1,0:T(8,128)(2,1)} %param.13) | copy-start | bytes 3440644
  7.2 164.4 %all-gather.15.cloned.1.call-start = ((), (), s32[]{:S(2)}) async-start(), calls=%async_computation.5 | async-start | bytes 3993600 | tf_op jit(solution)/shard_map/all_gather | solution.py:100
  43.4 253.7 %all-gather.13.cloned.1.call-start = ((), (), s32[]{:S(2)}) async-start(), calls=%async_computation.4 | async-start | bytes 5990400 | tf_op jit(solution)/shard_map/all_gather | solution.py:99
  79.3 339.5 %all-gather.11.cloned.1.call-start = ((), (), s32[]{:S(2)}) async-start(), calls=%async_computation.2 | async-start | bytes 2662400 | tf_op jit(solution)/shard_map/all_gather | solution.py:111
  80.9 411.5 %all-gather.9.cloned.1.call-start = ((), (), s32[]{:S(2)}) async-start(), calls=%async_computation.1 | async-start | bytes 2949120 | tf_op jit(solution)/shard_map/all_gather | solution.py:107
  177.7 127.0 %copy-start.2 = (bf16[1,128,1280]{2,1,0:T(8,128)(2,1)S(1)}, bf16[1,128,1280]{2,1,0:T(8,128)(2,1)}, u32[]{:S(2)}) copy-start(bf16[1,128,1280]{2,1,0:T(8,128)(2,1)} %param.8) | copy-start | bytes 983044
  177.7 127.0 %copy-start.3 = (f32[1280]{0:T(1024)S(1)}, f32[1280]{0:T(1024)}, u32[]{:S(2)}) copy-start(f32[1280]{0:T(1024)} %param.14) | copy-start | bytes 15364
  311.1 2.3 copy-start.1
  313.4 0.8 copy-start.4
  315.1 276.3 %reduce-scatter.2.cloned.1.call-start = ((), (), s32[]{:S(2)}) async-start(), calls=%async_computation.3 | async-start | bytes 2949120 | tf_op jit(solution)/shard_map/reduce_scatter | solution.py:115
Sparse Core Ops, SparseCore 0:
  43.5 128.0 all-gather.14
  174.3 122.7 all-gather.12
  299.3 119.4 all-gather.10
  422.4 69.9 all-gather.8
  500.7 90.5 reduce-scatter.1
where the time goes:
time: 601 us; the launch traced here: 600 us
  waiting for transfers between devices  468 us (78%)
  blocking collectives  68.8 us (11%)
  local copies, waits for them, and re-layouts  24.2 us (4%)
  matrix products  16.7 us (3%)
  between operations  14.6 us (2%)
  other arithmetic  7.37 us (1%)
    all_gather x1, waiting for transfers between devices, shards(): lax.all_gather(qkv_columns, 'group', axis=0, tiled=True)  119 us
    all_gather x1, waiting for transfers between devices, shards(): lax.all_gather(gate_up_master.astype(jnp.bfloat16), 'group', axis=0, tile...  104 us
    reduce_scatter x1, waiting for transfers between devices, shards(): lax.psum_scatter(jnp.dot(hidden_units, down_weight, preferred_element_typ...  89.9 us
    all_gather x1, waiting for transfers between devices, shards(): lax.all_gather(out_columns, 'group', axis=0, tiled=True)  88.6 us
    all_gather x1, waiting for transfers between devices, shards(): gathered_mid = lax.all_gather(normed_mid, 'shard', axis=0, tiled=True)  66.2 us
    all_gather x1, blocking collectives, shards(): lax.all_gather(out_master.astype(jnp.bfloat16), 'shard', axis=1, tiled=True)  34.6 us
    all_gather x1, blocking collectives, shards(): lax.all_gather(qkv_master.astype(jnp.bfloat16), 'shard', axis=1, tiled=True)  34.2 us
    unnamed x15, local copies, waits for them, and re-layouts  16.7 us
  transfers between devices with their start and end apart: 5, of which 5 were waited for; matrix products, arithmetic and copies ran while one was open for 6% of the time, Pallas kernels for 0%

commit v1 on v0

--- a/solution.py
+++ b/solution.py
@@ -104,7 +104,8 @@
     attended, rotated_keys, value_rows = attention(query_key_value, length)
     middle = stream + jnp.dot(attended, w_out, preferred_element_type=jnp.float32)
     normed_mid = norm_rows(middle, mlp_gain).astype(jnp.bfloat16)
-    gathered_mid = lax.all_gather(normed_mid, "shard", axis=0, tiled=True)
+    sent = jnp.stack([normed_mid] * lax.axis_size("shard"))
+    gathered_mid = jnp.concatenate(lax.all_to_all(sent, "shard", 0, 0), axis=0)
     units = gate_up_master.shape[2]
     summed_units = fold_units(
         gathered_mid,

time: 601 us -> 533 us (0.89)
  the two profiles are of different devices: /device:TPU:32 before, /device:TPU:8 now
where the time goes in v1:
time: 533 us; the launch traced here: 532 us
  waiting for transfers between devices  389 us (73%)
  blocking collectives  71.6 us (13%)
  local copies, waits for them, and re-layouts  25.9 us (5%)
  matrix products  16.7 us (3%)
  between operations  14.6 us (3%)
  starting transfers between devices  7.21 us (1%)
  other arithmetic  6.65 us (1%)
    all_gather x1, waiting for transfers between devices, shards(): lax.all_gather(qkv_columns, 'group', axis=0, tiled=True)  120 us
    all_gather x1, waiting for transfers between devices, shards(): lax.all_gather(gate_up_master.astype(jnp.bfloat16), 'group', axis=0, tile...  95.5 us
    reduce_scatter x1, waiting for transfers between devices, shards(): lax.psum_scatter(jnp.dot(hidden_units, down_weight, preferred_element_typ...  87.7 us
    all_gather x1, waiting for transfers between devices, shards(): lax.all_gather(out_columns, 'group', axis=0, tiled=True)  86 us
    all_gather x1, blocking collectives, shards(): lax.all_gather(out_master.astype(jnp.bfloat16), 'shard', axis=1, tiled=True)  37.4 us
    all_gather x1, blocking collectives, shards(): lax.all_gather(qkv_master.astype(jnp.bfloat16), 'shard', axis=1, tiled=True)  34.3 us
    unnamed x15, local copies, waits for them, and re-layouts  16.6 us
  transfers between devices with their start and end apart: 5, of which 4 were waited for; matrix products, arithmetic and copies ran while one was open for 7% of the time, Pallas kernels for 0%

profile of v1, /device:TPU:8, one launch (start us, length us, event | category | flops | bytes accessed | tf_op | source)
XLA Modules:
  0.0 531.7 jit_solution(4253616202569571463)
XLA Ops:
  7.2 0.8 convert_bitcast_fusion
  8.1 37.4 %all-gather.2 = bf16[8,160,20]{1,2,0:T(8,128)(2,1)S(1)} all-gather(bf16[1,160,20]{1,2,0:T(8,128)(2,1)S(1)} %convert_bitcast_fusion), channel_id=1, replica_groups=mesh['group'=64,'shard'=8] {'shard'}, dimensions={0}, use_global_device_ids=true | all-gather | bytes 57600 | tf_op jit(solution)/shard_map/all_gather | solution.py:94
  45.4 0.8 reshape.201
  46.2 0.0 all-gather.10.cloned.1.call-start
  46.3 0.7 convert_bitcast_fusion.1
  47.0 34.3 %all-gather = bf16[8,240,20]{1,2,0:T(8,128)(2,1)S(1)} all-gather(bf16[1,240,20]{1,2,0:T(8,128)(2,1)S(1)} %convert_bitcast_fusion.1), channel_id=1, replica_groups=mesh['group'=64,'shard'=8] {'shard'}, dimensions={0}, use_global_device_ids=true | all-gather | bytes 86400 | tf_op jit(solution)/shard_map/all_gather | solution.py:93
  81.3 0.8 reshape.197
  82.2 1.5 convert_element_type.147
  83.8 1.1 fusion.11
  85.6 0.1 fusion.32
  85.7 0.1 multiply_cosine_fusion
  85.8 86.0 %all-gather.12.cloned.1.call-done = bf16[64,20,1280]{2,1,0:T(8,128)(2,1)} async-done(((bf16[1,20,1280]{2,1,0:T(8,128)(2,1)}), bf16[64,20,1280]{2,1,0:T(8,128)(2,1)}) %all-gather.12.cloned.1.call-update) | async-done | bytes 3276816 | tf_op jit(solution)/shard_map/all_gather | solution.py:100
  171.8 6.1 %reshape.203 = bf16[1280,1280]{1,0:T(8,128)(2,1)} reshape(bf16[64,20,1280]{2,1,0:T(8,128)(2,1)} %all-gather.12.cloned.1.call-done) | data formatting | bytes 6553600
  177.9 119.7 %all-gather.10.cloned.1.call-done = bf16[64,20,1920]{2,1,0:T(8,128)(2,1)} async-done(((bf16[1,20,1920]{2,1,0:T(8,128)(2,1)}), bf16[64,20,1920]{2,1,0:T(8,128)(2,1)}) %all-gather.10.cloned.1.call-update) | async-done | bytes 4915216 | tf_op jit(solution)/shard_map/all_gather | solution.py:99
  297.7 7.5 %reshape.199 = bf16[1280,1920]{1,0:T(8,128)(2,1)} reshape(bf16[64,20,1920]{2,1,0:T(8,128)(2,1)} %all-gather.10.cloned.1.call-done) | data formatting | bytes 9830400
  305.2 4.4 convolution_convert_fusion.1
  309.7 0.1 convert.18
  309.8 0.1 subtract_convert_fusion
  309.9 1.7 fusion.40
  311.6 1.7 convolution_convert_fusion.2
  313.3 0.6 copy-done.1
  314.0 0.7 multiply_reduce_fusion
  314.7 0.1 multiply_convert_fusion.1
  314.9 1.7 stack.2
  316.5 7.1 %all-to-all-start = ((bf16[8,128,1280]{2,1,0:T(8,128)(2,1)}), bf16[8,128,1280]{2,1,0:T(8,128)(2,1)}, u32[]{:S(2)}, u32[]{:S(2)}) async-start(bf16[8,128,1280]{2,1,0:T(8,128)(2,1)} %stack.2), calls=%async_computation | async-start | bytes 5242880 | tf_op jit(solution)/shard_map/all_to_all | solution.py:108
  323.6 95.5 %all-gather.8.cloned.1.call-done = bf16[1280,2,448]{2,1,0:T(2,128)(2,1)} async-done(((bf16[20,2,448]{2,1,0:T(2,128)(2,1)}), bf16[1280,2,448]{2,1,0:T(2,128)(2,1)}) %all-gather.8.cloned.1.call-update) | async-done | bytes 2293776 | tf_op jit(solution)/shard_map/all_gather | solution.py:112
  419.1 7.5 %copy.40 = bf16[1280,2,448]{0,2,1:T(8,128)(2,1)} copy(bf16[1280,2,448]{2,1,0:T(2,128)(2,1)} %all-gather.8.cloned.1.call-done) | data formatting | bytes 4587520 | tf_op jit(solution)/shard_map/all_gather | solution.py:112
  426.6 5.0 fusion.1
  431.6 3.2 convolution_convert_fusion
  434.9 0.8 copy.41
  435.7 87.7 %reduce-scatter.2.cloned.1.call-done = bf16[128,1280]{1,0:T(8,128)(2,1)} async-done(((bf16[1024,1280]{1,0:T(8,128)(2,1)}), bf16[128,1280]{1,0:T(8,128)(2,1)}) %reduce-scatter.2.cloned.1.call-update) | async-done | bytes 327696 | tf_op jit(solution)/shard_map/reduce_scatter | solution.py:116
  523.4 1.8 fusion.14
  (31 shorter events, 0.4 us)
Async XLA Ops:
  7.2 424.4 %copy-start = (bf16[448,1280]{1,0:T(8,128)(2,1)S(1)}, bf16[448,1280]{1,0:T(8,128)(2,1)}, u32[]{:S(2)}) copy-start(bf16[448,1280]{1,0:T(8,128)(2,1)} %param.13) | copy-start | bytes 3440644
  7.2 164.7 %all-gather.12.cloned.1.call-start = ((), (), s32[]{:S(2)}) async-start(), calls=%async_computation.5 | async-start | bytes 3993600 | tf_op jit(solution)/shard_map/all_gather | solution.py:100
  46.2 251.5 %all-gather.10.cloned.1.call-start = ((), (), s32[]{:S(2)}) async-start(), calls=%async_computation.4 | async-start | bytes 5990400 | tf_op jit(solution)/shard_map/all_gather | solution.py:99
  82.1 337.0 %all-gather.8.cloned.1.call-start = ((), (), s32[]{:S(2)}) async-start(), calls=%async_computation.2 | async-start | bytes 2662400 | tf_op jit(solution)/shard_map/all_gather | solution.py:112
  177.9 127.3 %copy-start.2 = (bf16[1,128,1280]{2,1,0:T(8,128)(2,1)S(1)}, bf16[1,128,1280]{2,1,0:T(8,128)(2,1)}, u32[]{:S(2)}) copy-start(bf16[1,128,1280]{2,1,0:T(8,128)(2,1)} %param.8) | copy-start | bytes 983044
  177.9 127.3 %copy-start.3 = (f32[1280]{0:T(1024)S(1)}, f32[1280]{0:T(1024)}, u32[]{:S(2)}) copy-start(f32[1280]{0:T(1024)} %param.14) | copy-start | bytes 15364
  311.6 2.3 copy-start.1
  314.0 0.8 copy-start.4
  316.5 110.0 %all-to-all-start = ((bf16[8,128,1280]{2,1,0:T(8,128)(2,1)}), bf16[8,128,1280]{2,1,0:T(8,128)(2,1)}, u32[]{:S(2)}, u32[]{:S(2)}) async-start(bf16[8,128,1280]{2,1,0:T(8,128)(2,1)} %stack.2), calls=%async_computation | async-start | bytes 5242880 | tf_op jit(solution)/shard_map/all_to_all | solution.py:108
  323.6 199.8 %reduce-scatter.2.cloned.1.call-start = ((), (), s32[]{:S(2)}) async-start(), calls=%async_computation.3 | async-start | bytes 2949120 | tf_op jit(solution)/shard_map/reduce_scatter | solution.py:116
Sparse Core Ops, SparseCore 0:
  46.3 125.4 all-gather.11
  174.6 123.0 all-gather.9
  299.9 119.2 all-gather.7
  434.9 88.4 reduce-scatter.1
